TPU v7x, 128 devices: a whole 4x4x4 slice. The times are simulated.
128 devices in a mesh: basis: 16 (over x, z_lo, core), orb: 8 (over z_hi, y).
Axes of the slice: x: 4, y: 4, z: 4 (z_hi: 2, z_lo: 2; z = z_hi * 2 + z_lo), core: 2. Of those that a mesh axis runs over, the one named last changes fastest.
Arguments:
- cont_orbitals: bfloat16 [65536, 2048], P('basis', 'orb'), may hold values from -6 to 6
- target_orbitals: bfloat16 [65536, 1024], P('basis'), may hold values from -0.09375 to 0.09375
- margin_blocks: bfloat16 [256, 4, 256, 256], P('basis'), may hold values from -0.1875 to 0.1875
- dipole_blocks: bfloat16 [256, 4, 256, 256], P('basis'), may hold values from -0.1875 to 0.1875
- band_offsets: int32 [256, 4], P('basis'), may hold values from -2 to 2, as said below
Outputs:
- cont_orth: bfloat16 [65536, 2048], P('basis', 'orb')
- dipole_mo: bfloat16 [1024, 2048], P('basis', 'orb')
Inputs may be any that keep to these rules, and one draw needn't show every extreme that they name: `band_offsets`: each block row names 4 different offsets.
All inputs are finite; a program needn't handle non-finite values.
Results may differ from a plain program's by a relative error of at most 0.012.
Values may be sent and summed in bfloat16 or wider, within the bound.
A program may use at most 128 MiB of HBM per device.

v0:
```python
import jax
import jax.numpy as jnp
from jax import lax
from jax.sharding import PartitionSpec as P

BK = 256
KB = 4


def padded_2(block, sides, width):
    for axis, dim in sides:
        count = lax.axis_size(axis)
        forward = [(i, i + 1) for i in range(count - 1)]
        backward = [(target, source) for source, target in forward]
        low = lax.ppermute(
            lax.slice_in_dim(block, block.shape[dim] - width, None, axis=dim), axis, forward
        )
        high = lax.ppermute(lax.slice_in_dim(block, 0, width, axis=dim), axis, backward)
        block = jnp.concatenate([low, block, high], axis=dim)
    return block


def band_local(blocks, offsets, padded):
    nblk = blocks.shape[0]
    width = padded.shape[1]
    stacked = padded.reshape(nblk + 4, BK, width)
    total = jnp.zeros((nblk, BK, width), jnp.float32)
    for k in range(KB):
        index = jnp.arange(nblk, dtype=jnp.int32) + 2 + offsets[:, k]
        taken = stacked[index]
        total = total + jnp.einsum(
            "bij,bjc->bic", blocks[:, k], taken, preferred_element_type=jnp.float32
        )
    return total.reshape(nblk * BK, width)


def on_device(cont_orbitals, target_orbitals, margin_blocks, dipole_blocks, band_offsets):
    cont_padded = padded_2(cont_orbitals, (("basis", 0),), 2 * BK)
    margin_cont = band_local(margin_blocks, band_offsets, cont_padded).astype(jnp.bfloat16)
    partial_proj = lax.dot_general(
        target_orbitals, margin_cont, (((0,), (0,)), ((), ())), preferred_element_type=jnp.float32
    )
    projection = lax.psum(partial_proj, "basis")
    projection_b = projection.astype(jnp.bfloat16)
    removed = jnp.dot(target_orbitals, projection_b, preferred_element_type=jnp.float32)
    cont_orth = (cont_orbitals.astype(jnp.float32) - removed).astype(jnp.bfloat16)
    squares = jnp.sum(jnp.square(cont_orth.astype(jnp.float32)), axis=0)
    orth_padded = padded_2(cont_orth, (("basis", 0),), 2 * BK)
    total_squares = lax.psum(squares, "basis")
    col_norm = 1.0 / jnp.sqrt(
        total_squares / (band_offsets.shape[0] * BK * lax.axis_size("basis")) + 1e-06
    )
    dipole_cont = band_local(dipole_blocks, band_offsets, orth_padded).astype(jnp.bfloat16)
    dipole_raw = lax.psum_scatter(
        lax.dot_general(
            target_orbitals,
            dipole_cont,
            (((0,), (0,)), ((), ())),
            preferred_element_type=jnp.float32,
        ),
        "basis",
        scatter_dimension=0,
        tiled=True,
    )
    dipole_mo = (dipole_raw * col_norm[None, :]).astype(jnp.bfloat16)
    return (cont_orth, dipole_mo)


def solution(mesh):
    return jax.shard_map(
        on_device,
        mesh=mesh,
        in_specs=(
            P("basis", "orb"),
            P("basis", None),
            P("basis", None, None, None),
            P("basis", None, None, None),
            P("basis", None),
        ),
        out_specs=(P("basis", "orb"), P("basis", "orb")),
        check_vma=False,
    )
```

profile of v0, /device:TPU:0, one launch (start us, length us, event | category | flops | bytes accessed | tf_op | source)
XLA Modules:
  0.0 222.3 jit_solution(11804426336611701205)
XLA Ops:
  7.2 0.0 reduce-scatter.4.cloned.1.call-start
  7.2 1.1 fusion.30
  8.3 1.3 collective-permute-start
  9.6 1.3 collective-permute-start.1
  10.9 0.8 fusion.28
  11.7 4.1 %copy.30 = bf16[4096,256]{0,1:T(8,128)(2,1)} copy(bf16[4096,256]{1,0:T(8,128)(2,1)} %param.5) | data formatting | bytes 4194304 | tf_op args[0]
  15.9 0.0 collective-permute-done
  15.9 0.0 collective-permute-done.1
  15.9 1.8 pad_maximum_fusion
  17.6 2.0 gather_fusion.3
  19.6 2.0 gather_fusion.2
  21.6 2.0 gather_fusion.1
  23.7 2.0 gather_fusion
  25.7 3.1 %fusion.10 = f32[16,256,256]{1,2,0:T(8,128)S(1)} fusion(bf16[16,256,256]{2,1,0:T(8,128)(2,1)} %gather_fusion.2, bf16[16,4,256,256]{3,2,1,0:T(8,128)(2,1)} %param.7), kind=kOutput, calls=%fused_computation.24 | convolution fusion | flops 536870912 | bytes 8388608 | tf_op jit(solution)/shard_map/bij,bjc->bic/dot_general | solution.py:31
  28.8 0.0 copy-done.7
  28.8 0.0 copy-start.5
  28.8 2.5 %fusion.14 = f32[16,256,256]{1,2,0:T(8,128)S(1)} fusion(bf16[16,256,256]{2,1,0:T(8,128)(2,1)S(1)} %copy-done.7, bf16[16,4,256,256]{3,2,1,0:T(8,128)(2,1)} %param.7), kind=kOutput, calls=%fused_computation.28 | convolution fusion | flops 536870912 | bytes 8388608 | tf_op jit(solution)/shard_map/bij,bjc->bic/dot_general | solution.py:31
  31.3 0.0 copy-done.5
  31.3 0.0 copy-start.3
  31.3 0.0 slice-start
  31.3 2.5 %fusion.12 = f32[16,256,256]{1,2,0:T(8,128)S(1)} fusion(bf16[16,256,256]{2,1,0:T(8,128)(2,1)S(1)} %copy-done.5, bf16[16,4,256,256]{3,2,1,0:T(8,128)(2,1)} %param.7), kind=kOutput, calls=%fused_computation.26 | convolution fusion | flops 536870912 | bytes 8388608 | tf_op jit(solution)/shard_map/bij,bjc->bic/dot_general | solution.py:31
  33.8 0.0 copy-done.3
  33.8 0.0 slice-start.1
  33.8 3.0 %add_convert_fusion.1 = bf16[16,256,256]{1,2,0:T(8,128)(2,1)S(1)} fusion(f32[16,256,256]{1,2,0:T(8,128)S(1)} %fusion.10, f32[16,256,256]{1,2,0:T(8,128)S(1)} %fusion.14, f32[16,256,256]{1,2,0:T(8,128)S(1)} %fusion.12, bf16[16,256,256]{2,1,0:T(8,128)(2,1)S(1)} %copy-done.3, bf16[16,4,256,256]{3,2,1,0:T(8,128)(2,1)} %param.7), kind=kOutput, calls=%fused_computation.13 | convolution fusion | flops 541065216 | bytes 18874368 | tf_op jit(solution)/shard_map/bij,bjc->bic/dot_general | solution.py:31
  36.8 0.0 slice-done
  36.8 0.1 slice-done.1
  36.9 2.3 %convolution_bitcast_fusion.2 = f32[1024,256]{0,1:T(8,128)S(1)} fusion(bf16[4096,256]{1,0:T(8,128)(2,1)S(1)} %bitcast.93, bf16[4096,1024]{1,0:T(8,128)(2,1)S(1)} %bitcast.82), kind=kOutput, calls=%fused_computation.39 | convolution fusion | flops 2147483648 | bytes 11534336 | tf_op jit(solution)/shard_map/dot_general | solution.py:40
  39.2 70.3 %all-reduce.1 = bf16[1024,256]{0,1:T(8,128)(2,1)} all-reduce(f32[1024,256]{0,1:T(8,128)S(1)} %convolution_bitcast_fusion.2), channel_id=1, replica_groups=mesh['basis'=16,'orb'=8] {'basis'}, use_global_device_ids=true, to_apply=%region_0.0 | all-reduce | flops 262144 | bytes 1572864 | tf_op jit(solution)/shard_map/psum | solution.py:43
  109.6 0.0 copy-done.8
  109.6 6.2 %multiply_reduce_fusion = (f32[256]{0:T(256)S(1)}, bf16[4096,256]{0,1:T(8,128)(2,1)S(1)}) fusion(bf16[1024,256]{0,1:T(8,128)(2,1)} %all-reduce.1, bf16[4096,1024]{1,0:T(8,128)(2,1)} %param.6, bf16[4096,256]{0,1:T(8,128)(2,1)S(1)} %copy-done.8), kind=kOutput, calls=%fused_computation.11 | convolution fusion | flops 2153774848 | bytes 13108224 | tf_op jit(solution)/shard_map/dot_general | solution.py:45
  115.8 0.0 copy-start
  115.8 1.3 collective-permute-start.2
  117.2 1.5 collective-permute-start.3
  118.6 0.0 collective-permute-done.2
  118.6 1.9 collective-permute-done.3
  120.6 1.7 pad_maximum_fusion.1
  122.3 3.0 %copy.35 = bf16[5120,256]{1,0:T(8,128)(2,1)S(1)} copy(bf16[5120,256]{0,1:T(8,128)(2,1)} %pad_maximum_fusion.1) | data formatting | bytes 5242880 | tf_op jit(solution)/shard_map/concatenate | solution.py:19
  125.3 2.0 gather_fusion.7
  127.3 2.0 gather_fusion.6
  129.3 2.0 gather_fusion.5
  131.4 2.0 gather_fusion.4
  133.4 3.1 %fusion.7 = f32[16,256,256]{1,2,0:T(8,128)S(1)} fusion(bf16[16,256,256]{2,1,0:T(8,128)(2,1)} %gather_fusion.4, bf16[16,4,256,256]{3,2,1,0:T(8,128)(2,1)} %param.8), kind=kOutput, calls=%fused_computation.21 | convolution fusion | flops 536870912 | bytes 8388608 | tf_op jit(solution)/shard_map/bij,bjc->bic/dot_general | solution.py:31
  136.5 0.0 copy-done.6
  136.5 0.0 copy-start.4
  136.5 2.5 %fusion.5 = f32[16,256,256]{1,2,0:T(8,128)S(1)} fusion(bf16[16,256,256]{2,1,0:T(8,128)(2,1)S(1)} %copy-done.6, bf16[16,4,256,256]{3,2,1,0:T(8,128)(2,1)} %param.8), kind=kOutput, calls=%fused_computation.19 | convolution fusion | flops 536870912 | bytes 8388608 | tf_op jit(solution)/shard_map/bij,bjc->bic/dot_general | solution.py:31
  139.0 0.0 copy-done.4
  139.0 0.0 copy-start.2
  139.0 0.0 slice-start.2
  139.0 2.5 %fusion.3 = f32[16,256,256]{1,2,0:T(8,128)S(1)} fusion(bf16[16,256,256]{2,1,0:T(8,128)(2,1)S(1)} %copy-done.4, bf16[16,4,256,256]{3,2,1,0:T(8,128)(2,1)} %param.8), kind=kOutput, calls=%fused_computation.17 | convolution fusion | flops 536870912 | bytes 8388608 | tf_op jit(solution)/shard_map/bij,bjc->bic/dot_general | solution.py:31
  141.5 0.0 copy-done.2
  141.5 0.0 slice-start.3
  141.5 3.0 %add_convert_fusion = bf16[16,256,256]{1,2,0:T(8,128)(2,1)S(1)} fusion(f32[16,256,256]{1,2,0:T(8,128)S(1)} %fusion.3, f32[16,256,256]{1,2,0:T(8,128)S(1)} %fusion.7, f32[16,256,256]{1,2,0:T(8,128)S(1)} %fusion.5, bf16[16,256,256]{2,1,0:T(8,128)(2,1)S(1)} %copy-done.2, bf16[16,4,256,256]{3,2,1,0:T(8,128)(2,1)} %param.8), kind=kOutput, calls=%fused_computation.12 | convolution fusion | flops 541065216 | bytes 18874368 | tf_op jit(solution)/shard_map/bij,bjc->bic/dot_general | solution.py:31
  144.5 0.1 slice-done.3
  144.6 2.3 %convolution_bitcast_fusion.1 = f32[1024,256]{0,1:T(8,128)S(1)} fusion(bf16[4096,256]{1,0:T(8,128)(2,1)S(1)} %bitcast.94, bf16[4096,1024]{1,0:T(8,128)(2,1)S(1)} %bitcast.84), kind=kOutput, calls=%fused_computation.38 | convolution fusion | flops 2147483648 | bytes 11534336 | tf_op jit(solution)/shard_map/dot_general | solution.py:55
  146.9 0.0 copy-start.1
  146.9 1.3 copy.42
  148.2 0.0 reduce-scatter.4.cloned.1.call-update
  148.3 0.6 copy-done.1
  148.9 2.4 %copy.40 = bf16[4096,256]{1,0:T(8,128)(2,1)} copy(bf16[4096,256]{0,1:T(8,128)(2,1)S(1)} %copy-done.1) | data formatting | bytes 4194304
  151.3 29.2 %psum.15 = f32[256]{0:T(256)S(1)} all-reduce(f32[256]{0:T(256)S(1)} %get-tuple-element.16), channel_id=1, replica_groups=mesh['basis'=16,'orb'=8] {'basis'}, use_global_device_ids=true, to_apply=%region_3.0 | all-reduce | flops 256 | bytes 2048 | tf_op jit(solution)/shard_map/psum | solution.py:49
  180.5 33.2 %reduce-scatter.4.cloned.1.call-done = f32[64,256]{1,0:T(8,128)} async-done(((f32[1024,256]{1,0:T(8,128)}), f32[64,256]{1,0:T(8,128)}) %reduce-scatter.4.cloned.1.call-update) | async-done | bytes 65552
  213.7 0.9 copy.43
  214.7 0.1 multiply_convert_fusion
  214.8 0.7 copy.41
  (11 shorter events, 0.1 us)
Async XLA Ops:
  7.2 206.6 %reduce-scatter.4.cloned.1.call-start = ((), (), s32[]{:S(2)}) async-start(), calls=%async_computation.1 | async-start | bytes 1114112
  8.3 7.6 %collective-permute-start = (bf16[512,256]{1,0:T(8,128)(2,1)S(1)}, bf16[512,256]{1,0:T(8,128)(2,1)S(1)}, u32[]{:S(2)}, u32[]{:S(2)}) collective-permute-start(bf16[512,256]{1,0:T(8,128)(2,1)S(1)} %get-tuple-element.10), channel_id=1, source_target_pairs={{0,8},{8,16},{16,24},{24,32},{32,40},{40,48},{48,56},{56,64},{64,7... | collective-permute-start | bytes 786440 | tf_op jit(solution)/shard_map/ppermute | solution.py:15
  9.6 6.3 %collective-permute-start.1 = (bf16[512,256]{1,0:T(8,128)(2,1)S(1)}, bf16[512,256]{1,0:T(8,128)(2,1)S(1)}, u32[]{:S(2)}, u32[]{:S(2)}) collective-permute-start(bf16[512,256]{1,0:T(8,128)(2,1)S(1)} %get-tuple-element.11), channel_id=1, source_target_pairs={{8,0},{16,8},{24,16},{32,24},{40,32},{48,40},{56,48},{64,56},{72,6... | collective-permute-start | bytes 786440 | tf_op jit(solution)/shard_map/ppermute | solution.py:18
  25.7 3.1 %copy-start.7 = (bf16[16,256,256]{2,1,0:T(8,128)(2,1)S(1)}, bf16[16,256,256]{2,1,0:T(8,128)(2,1)}, u32[]{:S(2)}) copy-start(bf16[16,256,256]{2,1,0:T(8,128)(2,1)} %gather_fusion) | copy-start | bytes 6291460
  28.8 2.5 %copy-start.5 = (bf16[16,256,256]{2,1,0:T(8,128)(2,1)S(1)}, bf16[16,256,256]{2,1,0:T(8,128)(2,1)}, u32[]{:S(2)}) copy-start(bf16[16,256,256]{2,1,0:T(8,128)(2,1)} %gather_fusion.1) | copy-start | bytes 6291460
  31.3 2.5 %copy-start.3 = (bf16[16,256,256]{2,1,0:T(8,128)(2,1)S(1)}, bf16[16,256,256]{2,1,0:T(8,128)(2,1)}, u32[]{:S(2)}) copy-start(bf16[16,256,256]{2,1,0:T(8,128)(2,1)} %gather_fusion.3) | copy-start | bytes 6291460
  31.3 5.5 %slice-start = ((s8[8388608]{0:T(1024)(128)(4,1)}), s8[4194304]{0:T(1024)(128)(4,1)S(1)}, s32[]{:S(2)}) async-start(s8[8388608]{0:T(1024)(128)(4,1)} %bitcast.81), calls=%async_computation.2 | async-start | bytes 8388608
  33.8 3.1 %slice-start.1 = ((s8[8388608]{0:T(1024)(128)(4,1)}), s8[4194304]{0:T(1024)(128)(4,1)S(1)}, s32[]{:S(2)}) async-start(s8[8388608]{0:T(1024)(128)(4,1)} %bitcast.81), calls=%async_computation.3 | async-start | bytes 8388608
  36.9 72.7 %copy-start.8 = (bf16[4096,256]{0,1:T(8,128)(2,1)S(1)}, bf16[4096,256]{0,1:T(8,128)(2,1)}, u32[]{:S(2)}) copy-start(bf16[4096,256]{0,1:T(8,128)(2,1)} %copy.30) | copy-start | bytes 6291460
  115.8 4.8 %copy-start = (bf16[4096,256]{0,1:T(8,128)(2,1)}, bf16[4096,256]{0,1:T(8,128)(2,1)S(1)}, u32[]{:S(2)}) copy-start(bf16[4096,256]{0,1:T(8,128)(2,1)S(1)} %get-tuple-element.17) | copy-start | bytes 6291460
  115.8 2.8 %collective-permute-start.2 = (bf16[512,256]{0,1:T(8,128)(2,1)S(1)}, bf16[512,256]{0,1:T(8,128)(2,1)S(1)}, u32[]{:S(2)}, u32[]{:S(2)}) collective-permute-start(bf16[512,256]{0,1:T(8,128)(2,1)S(1)} %get-tuple-element.8), channel_id=1, source_target_pairs={{0,8},{8,16},{16,24},{24,32},{32,40},{40,48},{48,56},{56,64},{64,7... | collective-permute-start | bytes 786440 | tf_op jit(solution)/shard_map/ppermute | solution.py:15
  117.2 3.4 %collective-permute-start.3 = (bf16[512,256]{0,1:T(8,128)(2,1)S(1)}, bf16[512,256]{0,1:T(8,128)(2,1)S(1)}, u32[]{:S(2)}, u32[]{:S(2)}) collective-permute-start(bf16[512,256]{0,1:T(8,128)(2,1)S(1)} %get-tuple-element.9), channel_id=1, source_target_pairs={{8,0},{16,8},{24,16},{32,24},{40,32},{48,40},{56,48},{64,56},{72,6... | collective-permute-start | bytes 786440 | tf_op jit(solution)/shard_map/ppermute | solution.py:18
  133.4 3.1 %copy-start.6 = (bf16[16,256,256]{2,1,0:T(8,128)(2,1)S(1)}, bf16[16,256,256]{2,1,0:T(8,128)(2,1)}, u32[]{:S(2)}) copy-start(bf16[16,256,256]{2,1,0:T(8,128)(2,1)} %gather_fusion.5) | copy-start | bytes 6291460
  136.5 2.5 %copy-start.4 = (bf16[16,256,256]{2,1,0:T(8,128)(2,1)S(1)}, bf16[16,256,256]{2,1,0:T(8,128)(2,1)}, u32[]{:S(2)}) copy-start(bf16[16,256,256]{2,1,0:T(8,128)(2,1)} %gather_fusion.6) | copy-start | bytes 6291460
  139.0 2.5 %copy-start.2 = (bf16[16,256,256]{2,1,0:T(8,128)(2,1)S(1)}, bf16[16,256,256]{2,1,0:T(8,128)(2,1)}, u32[]{:S(2)}) copy-start(bf16[16,256,256]{2,1,0:T(8,128)(2,1)} %gather_fusion.7) | copy-start | bytes 6291460
  139.0 5.5 %slice-start.2 = ((s8[8388608]{0:T(1024)(128)(4,1)}), s8[4194304]{0:T(1024)(128)(4,1)S(1)}, s32[]{:S(2)}) async-start(s8[8388608]{0:T(1024)(128)(4,1)} %bitcast.83), calls=%async_computation.4 | async-start | bytes 8388608
  141.5 3.1 %slice-start.3 = ((s8[8388608]{0:T(1024)(128)(4,1)}), s8[4194304]{0:T(1024)(128)(4,1)S(1)}, s32[]{:S(2)}) async-start(s8[8388608]{0:T(1024)(128)(4,1)} %bitcast.83), calls=%async_computation.5 | async-start | bytes 8388608
  146.9 2.0 copy-start.1
Sparse Core Ops, SparseCore 0:
  148.4 65.3 reduce-scatter.3
where the time goes:
time: 223 us; the launch traced here: 222 us
  blocking collectives  99.5 us (45%)
  waiting for transfers between devices  35.2 us (16%)
  matrix products  32.8 us (15%)
  local copies, waits for them, and re-layouts  30.6 us (14%)
  between operations  14.3 us (6%)
  starting transfers between devices  5.41 us (2%)
  other arithmetic  4.47 us (2%)
    psum x1, blocking collectives, on_device(): projection = lax.psum(partial_proj, 'basis')  70.3 us
    unnamed x2, waiting for transfers between devices  33.2 us
    psum x1, blocking collectives, on_device(): total_squares = lax.psum(squares, 'basis')  29.2 us
    dot_general x8, matrix products, band_local(): jnp.einsum('bij,bjc->bic', blocks[:, k], taken, preferred_element_type=jn...  21.9 us
    gather x8, local copies, waits for them, and re-layouts, band_local(): taken = stacked[index]  16.2 us
    unnamed x31, local copies, waits for them, and re-layouts  10.3 us
    dot_general x1, matrix products, on_device(): jnp.dot(target_orbitals, projection_b, preferred_element_type=jnp.float32)  6.21 us
  transfers between devices with their start and end apart: 5, of which 2 were waited for; matrix products, arithmetic and copies ran while one was open for 3% of the time, Pallas kernels for 0%

commit v1 on v0

--- a/solution.py
+++ b/solution.py
@@ -46,7 +46,7 @@
     cont_orth = (cont_orbitals.astype(jnp.float32) - removed).astype(jnp.bfloat16)
     squares = jnp.sum(jnp.square(cont_orth.astype(jnp.float32)), axis=0)
     orth_padded = padded_2(cont_orth, (("basis", 0),), 2 * BK)
-    total_squares = lax.psum(squares, "basis")
+    total_squares = jnp.sum(lax.all_gather(squares, "basis"), axis=0)
     col_norm = 1.0 / jnp.sqrt(
         total_squares / (band_offsets.shape[0] * BK * lax.axis_size("basis")) + 1e-06
     )

time: 223 us -> 223 us (level)
  blocking collectives: 99.5 us -> 90.4 us
  waiting for transfers between devices: 35.2 us -> 44.2 us
    psum x1 -> x0, blocking collectives: 29.2 us -> none  [on_device(): total_squares = lax.psum(squares, 'basis')]
    all_gather x0 -> x1, blocking collectives: none -> 20.1 us  [on_device(): total_squares = jnp.sum(lax.all_gather(squares, 'basis'), axis=0)]
    unnamed x2, waiting for transfers between devices: 33.2 us -> 42.3 us
where the time goes in v1:
time: 223 us; the launch traced here: 222 us
  blocking collectives  90.4 us (41%)
  waiting for transfers between devices  44.2 us (20%)
  matrix products  32.8 us (15%)
  local copies, waits for them, and re-layouts  30.6 us (14%)
  between operations  14.3 us (6%)
  starting transfers between devices  5.41 us (2%)
  other arithmetic  4.5 us (2%)
    psum x1, blocking collectives, on_device(): projection = lax.psum(partial_proj, 'basis')  70.3 us
    unnamed x2, waiting for transfers between devices  42.3 us
    dot_general x8, matrix products, band_local(): jnp.einsum('bij,bjc->bic', blocks[:, k], taken, preferred_element_type=jn...  21.9 us
    all_gather x1, blocking collectives, on_device(): total_squares = jnp.sum(lax.all_gather(squares, 'basis'), axis=0)  20.1 us
    gather x8, local copies, waits for them, and re-layouts, band_local(): taken = stacked[index]  16.2 us
    unnamed x31, local copies, waits for them, and re-layouts  10.3 us
    dot_general x1, matrix products, on_device(): jnp.dot(target_orbitals, projection_b, preferred_element_type=jnp.float32)  6.21 us
  transfers between devices with their start and end apart: 5, of which 2 were waited for; matrix products, arithmetic and copies ran while one was open for 3% of the time, Pallas kernels for 0%

profile of v1, /device:TPU:0, one launch (start us, length us, event | category | flops | bytes accessed | tf_op | source)
XLA Modules:
  0.0 222.3 jit_solution(400602679498883476)
XLA Ops:
  7.2 0.0 reduce-scatter.4.cloned.1.call-start
  7.2 1.1 fusion.30
  8.3 1.3 collective-permute-start
  9.6 1.3 collective-permute-start.1
  10.9 0.8 fusion.28
  11.7 4.1 %copy.30 = bf16[4096,256]{0,1:T(8,128)(2,1)} copy(bf16[4096,256]{1,0:T(8,128)(2,1)} %param.5) | data formatting | bytes 4194304 | tf_op args[0]
  15.9 0.0 collective-permute-done
  15.9 0.0 collective-permute-done.1
  15.9 1.8 pad_maximum_fusion
  17.6 2.0 gather_fusion.3
  19.6 2.0 gather_fusion.2
  21.6 2.0 gather_fusion.1
  23.7 2.0 gather_fusion
  25.7 3.1 %fusion.10 = f32[16,256,256]{1,2,0:T(8,128)S(1)} fusion(bf16[16,256,256]{2,1,0:T(8,128)(2,1)} %gather_fusion.2, bf16[16,4,256,256]{3,2,1,0:T(8,128)(2,1)} %param.7), kind=kOutput, calls=%fused_computation.24 | convolution fusion | flops 536870912 | bytes 8388608 | tf_op jit(solution)/shard_map/bij,bjc->bic/dot_general | solution.py:31
  28.8 0.0 copy-done.7
  28.8 0.0 copy-start.5
  28.8 2.5 %fusion.14 = f32[16,256,256]{1,2,0:T(8,128)S(1)} fusion(bf16[16,256,256]{2,1,0:T(8,128)(2,1)S(1)} %copy-done.7, bf16[16,4,256,256]{3,2,1,0:T(8,128)(2,1)} %param.7), kind=kOutput, calls=%fused_computation.28 | convolution fusion | flops 536870912 | bytes 8388608 | tf_op jit(solution)/shard_map/bij,bjc->bic/dot_general | solution.py:31
  31.3 0.0 copy-done.5
  31.3 0.0 copy-start.3
  31.3 0.0 slice-start
  31.3 2.5 %fusion.12 = f32[16,256,256]{1,2,0:T(8,128)S(1)} fusion(bf16[16,256,256]{2,1,0:T(8,128)(2,1)S(1)} %copy-done.5, bf16[16,4,256,256]{3,2,1,0:T(8,128)(2,1)} %param.7), kind=kOutput, calls=%fused_computation.26 | convolution fusion | flops 536870912 | bytes 8388608 | tf_op jit(solution)/shard_map/bij,bjc->bic/dot_general | solution.py:31
  33.8 0.0 copy-done.3
  33.8 0.0 slice-start.1
  33.8 3.0 %add_convert_fusion.1 = bf16[16,256,256]{1,2,0:T(8,128)(2,1)S(1)} fusion(f32[16,256,256]{1,2,0:T(8,128)S(1)} %fusion.10, f32[16,256,256]{1,2,0:T(8,128)S(1)} %fusion.14, f32[16,256,256]{1,2,0:T(8,128)S(1)} %fusion.12, bf16[16,256,256]{2,1,0:T(8,128)(2,1)S(1)} %copy-done.3, bf16[16,4,256,256]{3,2,1,0:T(8,128)(2,1)} %param.7), kind=kOutput, calls=%fused_computation.13 | convolution fusion | flops 541065216 | bytes 18874368 | tf_op jit(solution)/shard_map/bij,bjc->bic/dot_general | solution.py:31
  36.8 0.0 slice-done
  36.8 0.1 slice-done.1
  36.9 2.3 %convolution_bitcast_fusion.2 = f32[1024,256]{0,1:T(8,128)S(1)} fusion(bf16[4096,256]{1,0:T(8,128)(2,1)S(1)} %bitcast.94, bf16[4096,1024]{1,0:T(8,128)(2,1)S(1)} %bitcast.83), kind=kOutput, calls=%fused_computation.39 | convolution fusion | flops 2147483648 | bytes 11534336 | tf_op jit(solution)/shard_map/dot_general | solution.py:40
  39.2 70.3 %all-reduce.1 = bf16[1024,256]{0,1:T(8,128)(2,1)} all-reduce(f32[1024,256]{0,1:T(8,128)S(1)} %convolution_bitcast_fusion.2), channel_id=1, replica_groups=mesh['basis'=16,'orb'=8] {'basis'}, use_global_device_ids=true, to_apply=%region_0.0 | all-reduce | flops 262144 | bytes 1572864 | tf_op jit(solution)/shard_map/psum | solution.py:43
  109.6 0.0 copy-done.8
  109.6 6.2 %multiply_reduce_fusion = (f32[256]{0:T(256)S(1)}, bf16[4096,256]{0,1:T(8,128)(2,1)S(1)}) fusion(bf16[1024,256]{0,1:T(8,128)(2,1)} %all-reduce.1, bf16[4096,1024]{1,0:T(8,128)(2,1)} %param.6, bf16[4096,256]{0,1:T(8,128)(2,1)S(1)} %copy-done.8), kind=kOutput, calls=%fused_computation.11 | convolution fusion | flops 2153774848 | bytes 13108224 | tf_op jit(solution)/shard_map/dot_general | solution.py:45
  115.8 0.0 copy-start
  115.8 1.3 collective-permute-start.2
  117.2 1.5 collective-permute-start.3
  118.6 0.0 collective-permute-done.2
  118.6 1.9 collective-permute-done.3
  120.6 1.7 pad_maximum_fusion.1
  122.3 3.0 %copy.35 = bf16[5120,256]{1,0:T(8,128)(2,1)S(1)} copy(bf16[5120,256]{0,1:T(8,128)(2,1)} %pad_maximum_fusion.1) | data formatting | bytes 5242880 | tf_op jit(solution)/shard_map/concatenate | solution.py:19
  125.3 2.0 gather_fusion.7
  127.3 2.0 gather_fusion.6
  129.3 2.0 gather_fusion.5
  131.4 2.0 gather_fusion.4
  133.4 3.1 %fusion.7 = f32[16,256,256]{1,2,0:T(8,128)S(1)} fusion(bf16[16,256,256]{2,1,0:T(8,128)(2,1)} %gather_fusion.4, bf16[16,4,256,256]{3,2,1,0:T(8,128)(2,1)} %param.8), kind=kOutput, calls=%fused_computation.21 | convolution fusion | flops 536870912 | bytes 8388608 | tf_op jit(solution)/shard_map/bij,bjc->bic/dot_general | solution.py:31
  136.5 0.0 copy-done.6
  136.5 0.0 copy-start.4
  136.5 2.5 %fusion.5 = f32[16,256,256]{1,2,0:T(8,128)S(1)} fusion(bf16[16,256,256]{2,1,0:T(8,128)(2,1)S(1)} %copy-done.6, bf16[16,4,256,256]{3,2,1,0:T(8,128)(2,1)} %param.8), kind=kOutput, calls=%fused_computation.19 | convolution fusion | flops 536870912 | bytes 8388608 | tf_op jit(solution)/shard_map/bij,bjc->bic/dot_general | solution.py:31
  139.0 0.0 copy-done.4
  139.0 0.0 copy-start.2
  139.0 0.0 slice-start.2
  139.0 2.5 %fusion.3 = f32[16,256,256]{1,2,0:T(8,128)S(1)} fusion(bf16[16,256,256]{2,1,0:T(8,128)(2,1)S(1)} %copy-done.4, bf16[16,4,256,256]{3,2,1,0:T(8,128)(2,1)} %param.8), kind=kOutput, calls=%fused_computation.17 | convolution fusion | flops 536870912 | bytes 8388608 | tf_op jit(solution)/shard_map/bij,bjc->bic/dot_general | solution.py:31
  141.5 0.0 copy-done.2
  141.5 0.0 slice-start.3
  141.5 3.0 %add_convert_fusion = bf16[16,256,256]{1,2,0:T(8,128)(2,1)S(1)} fusion(f32[16,256,256]{1,2,0:T(8,128)S(1)} %fusion.3, f32[16,256,256]{1,2,0:T(8,128)S(1)} %fusion.7, f32[16,256,256]{1,2,0:T(8,128)S(1)} %fusion.5, bf16[16,256,256]{2,1,0:T(8,128)(2,1)S(1)} %copy-done.2, bf16[16,4,256,256]{3,2,1,0:T(8,128)(2,1)} %param.8), kind=kOutput, calls=%fused_computation.12 | convolution fusion | flops 541065216 | bytes 18874368 | tf_op jit(solution)/shard_map/bij,bjc->bic/dot_general | solution.py:31
  144.5 0.1 slice-done.3
  144.6 2.3 %convolution_bitcast_fusion.1 = f32[1024,256]{0,1:T(8,128)S(1)} fusion(bf16[4096,256]{1,0:T(8,128)(2,1)S(1)} %bitcast.95, bf16[4096,1024]{1,0:T(8,128)(2,1)S(1)} %bitcast.85), kind=kOutput, calls=%fused_computation.38 | convolution fusion | flops 2147483648 | bytes 11534336 | tf_op jit(solution)/shard_map/dot_general | solution.py:55
  146.9 0.0 copy-start.1
  146.9 1.3 copy.42
  148.2 0.0 reduce-scatter.4.cloned.1.call-update
  148.3 0.6 copy-done.1
  148.9 2.4 %copy.40 = bf16[4096,256]{1,0:T(8,128)(2,1)} copy(bf16[4096,256]{0,1:T(8,128)(2,1)S(1)} %copy-done.1) | data formatting | bytes 4194304
  151.3 20.1 %all-gather.1 = f32[16,1,256]{2,1,0:T(1,128)S(1)} all-gather(f32[1,1,256]{2,1,0:T(1,128)S(1)} %bitcast.96), channel_id=2, replica_groups=mesh['basis'=16,'orb'=8] {'basis'}, dimensions={0}, use_global_device_ids=true | all-gather | bytes 17408 | tf_op jit(solution)/shard_map/all_gather | solution.py:49
  171.5 42.3 %reduce-scatter.4.cloned.1.call-done = f32[64,256]{1,0:T(8,128)} async-done(((f32[1024,256]{1,0:T(8,128)}), f32[64,256]{1,0:T(8,128)}) %reduce-scatter.4.cloned.1.call-update) | async-done | bytes 65552
  213.7 0.9 copy.43
  214.7 0.1 multiply_convert_fusion
  214.8 0.7 copy.41
  (12 shorter events, 0.1 us)
Async XLA Ops:
  7.2 206.6 %reduce-scatter.4.cloned.1.call-start = ((), (), s32[]{:S(2)}) async-start(), calls=%async_computation.1 | async-start | bytes 1114112
  8.3 7.6 %collective-permute-start = (bf16[512,256]{1,0:T(8,128)(2,1)S(1)}, bf16[512,256]{1,0:T(8,128)(2,1)S(1)}, u32[]{:S(2)}, u32[]{:S(2)}) collective-permute-start(bf16[512,256]{1,0:T(8,128)(2,1)S(1)} %get-tuple-element.10), channel_id=1, source_target_pairs={{0,8},{8,16},{16,24},{24,32},{32,40},{40,48},{48,56},{56,64},{64,7... | collective-permute-start | bytes 786440 | tf_op jit(solution)/shard_map/ppermute | solution.py:15
  9.6 6.3 %collective-permute-start.1 = (bf16[512,256]{1,0:T(8,128)(2,1)S(1)}, bf16[512,256]{1,0:T(8,128)(2,1)S(1)}, u32[]{:S(2)}, u32[]{:S(2)}) collective-permute-start(bf16[512,256]{1,0:T(8,128)(2,1)S(1)} %get-tuple-element.11), channel_id=1, source_target_pairs={{8,0},{16,8},{24,16},{32,24},{40,32},{48,40},{56,48},{64,56},{72,6... | collective-permute-start | bytes 786440 | tf_op jit(solution)/shard_map/ppermute | solution.py:18
  25.7 3.1 %copy-start.7 = (bf16[16,256,256]{2,1,0:T(8,128)(2,1)S(1)}, bf16[16,256,256]{2,1,0:T(8,128)(2,1)}, u32[]{:S(2)}) copy-start(bf16[16,256,256]{2,1,0:T(8,128)(2,1)} %gather_fusion) | copy-start | bytes 6291460
  28.8 2.5 %copy-start.5 = (bf16[16,256,256]{2,1,0:T(8,128)(2,1)S(1)}, bf16[16,256,256]{2,1,0:T(8,128)(2,1)}, u32[]{:S(2)}) copy-start(bf16[16,256,256]{2,1,0:T(8,128)(2,1)} %gather_fusion.1) | copy-start | bytes 6291460
  31.3 2.5 %copy-start.3 = (bf16[16,256,256]{2,1,0:T(8,128)(2,1)S(1)}, bf16[16,256,256]{2,1,0:T(8,128)(2,1)}, u32[]{:S(2)}) copy-start(bf16[16,256,256]{2,1,0:T(8,128)(2,1)} %gather_fusion.3) | copy-start | bytes 6291460
  31.3 5.5 %slice-start = ((s8[8388608]{0:T(1024)(128)(4,1)}), s8[4194304]{0:T(1024)(128)(4,1)S(1)}, s32[]{:S(2)}) async-start(s8[8388608]{0:T(1024)(128)(4,1)} %bitcast.82), calls=%async_computation.2 | async-start | bytes 8388608
  33.8 3.1 %slice-start.1 = ((s8[8388608]{0:T(1024)(128)(4,1)}), s8[4194304]{0:T(1024)(128)(4,1)S(1)}, s32[]{:S(2)}) async-start(s8[8388608]{0:T(1024)(128)(4,1)} %bitcast.82), calls=%async_computation.3 | async-start | bytes 8388608
  36.9 72.7 %copy-start.8 = (bf16[4096,256]{0,1:T(8,128)(2,1)S(1)}, bf16[4096,256]{0,1:T(8,128)(2,1)}, u32[]{:S(2)}) copy-start(bf16[4096,256]{0,1:T(8,128)(2,1)} %copy.30) | copy-start | bytes 6291460
  115.8 4.8 %copy-start = (bf16[4096,256]{0,1:T(8,128)(2,1)}, bf16[4096,256]{0,1:T(8,128)(2,1)S(1)}, u32[]{:S(2)}) copy-start(bf16[4096,256]{0,1:T(8,128)(2,1)S(1)} %get-tuple-element.17) | copy-start | bytes 6291460
  115.8 2.8 %collective-permute-start.2 = (bf16[512,256]{0,1:T(8,128)(2,1)S(1)}, bf16[512,256]{0,1:T(8,128)(2,1)S(1)}, u32[]{:S(2)}, u32[]{:S(2)}) collective-permute-start(bf16[512,256]{0,1:T(8,128)(2,1)S(1)} %get-tuple-element.8), channel_id=1, source_target_pairs={{0,8},{8,16},{16,24},{24,32},{32,40},{40,48},{48,56},{56,64},{64,7... | collective-permute-start | bytes 786440 | tf_op jit(solution)/shard_map/ppermute | solution.py:15
  117.2 3.4 %collective-permute-start.3 = (bf16[512,256]{0,1:T(8,128)(2,1)S(1)}, bf16[512,256]{0,1:T(8,128)(2,1)S(1)}, u32[]{:S(2)}, u32[]{:S(2)}) collective-permute-start(bf16[512,256]{0,1:T(8,128)(2,1)S(1)} %get-tuple-element.9), channel_id=1, source_target_pairs={{8,0},{16,8},{24,16},{32,24},{40,32},{48,40},{56,48},{64,56},{72,6... | collective-permute-start | bytes 786440 | tf_op jit(solution)/shard_map/ppermute | solution.py:18
  133.4 3.1 %copy-start.6 = (bf16[16,256,256]{2,1,0:T(8,128)(2,1)S(1)}, bf16[16,256,256]{2,1,0:T(8,128)(2,1)}, u32[]{:S(2)}) copy-start(bf16[16,256,256]{2,1,0:T(8,128)(2,1)} %gather_fusion.5) | copy-start | bytes 6291460
  136.5 2.5 %copy-start.4 = (bf16[16,256,256]{2,1,0:T(8,128)(2,1)S(1)}, bf16[16,256,256]{2,1,0:T(8,128)(2,1)}, u32[]{:S(2)}) copy-start(bf16[16,256,256]{2,1,0:T(8,128)(2,1)} %gather_fusion.6) | copy-start | bytes 6291460
  139.0 2.5 %copy-start.2 = (bf16[16,256,256]{2,1,0:T(8,128)(2,1)S(1)}, bf16[16,256,256]{2,1,0:T(8,128)(2,1)}, u32[]{:S(2)}) copy-start(bf16[16,256,256]{2,1,0:T(8,128)(2,1)} %gather_fusion.7) | copy-start | bytes 6291460
  139.0 5.5 %slice-start.2 = ((s8[8388608]{0:T(1024)(128)(4,1)}), s8[4194304]{0:T(1024)(128)(4,1)S(1)}, s32[]{:S(2)}) async-start(s8[8388608]{0:T(1024)(128)(4,1)} %bitcast.84), calls=%async_computation.4 | async-start | bytes 8388608
  141.5 3.1 %slice-start.3 = ((s8[8388608]{0:T(1024)(128)(4,1)}), s8[4194304]{0:T(1024)(128)(4,1)S(1)}, s32[]{:S(2)}) async-start(s8[8388608]{0:T(1024)(128)(4,1)} %bitcast.84), calls=%async_computation.5 | async-start | bytes 8388608
  146.9 2.0 copy-start.1
Sparse Core Ops, SparseCore 0:
  148.4 65.2 reduce-scatter.3
